TPU v7x, 256 devices: a whole 4x4x8 slice. The times are simulated.
256 devices in a mesh: row: 16 (over y, x), col: 16 (over z, core).
Axes of the slice: x: 4, y: 4, z: 8, core: 2. Of those that a mesh axis runs over, the one named last changes fastest.
Arguments:
- block_values: float32 [16, 16, 40, 128, 128], P('row', 'col'), may hold values from 7.8125e-06 to 0.00078125
- block_index: int32 [16, 16, 2, 40], P('row', 'col'), may hold values from 0 to 31, as said below
- block_count: int32 [16, 16], P('row', 'col'), may hold values from 1 to 40, as said below
- strength: float32 [32], replicated, may hold values from 1 to 30
- raw_scores: float32 [512, 32, 128], P(('row', 'col')), may hold values from -24 to 24
Outputs:
- smoothed: float32 [512, 32, 128], P(('row', 'col'))
- final_residual: float32 [512, 32, 128], P(('row', 'col'))
Inputs may be any that keep to these rules, and one draw needn't show every extreme that they name: `block_count`: some device has exactly 40 live slots; the others hold between half and all of their share of the upper triangle, scaled to 40. `block_index`: the live slots of one device name distinct blocks, each with global block row at most its global block column; slots at or above the count hold pairs in range that are ignored.
All inputs are finite; a program needn't handle non-finite values.
Results may differ from a plain program's by a relative error of at most 0.0003.
Values sent between devices are 32-bit elements; how exact they have to be, the bound alone decides.
A program may use at most 64 MiB of HBM per device.

v0:
```python
import jax
import jax.numpy as jnp
from jax import lax
from jax.sharding import PartitionSpec as P

ITERS = 3


def local_terms(values, row_index, col_index, panel_rows, panel_cols):
    picked_cols = jnp.take(panel_cols, col_index, axis=0)
    picked_rows = jnp.take(panel_rows, row_index, axis=0)
    to_rows = jnp.einsum("crk,cik->cri", picked_cols, values, precision=lax.Precision.HIGHEST)
    to_cols = jnp.einsum("cri,cik->crk", picked_rows, values, precision=lax.Precision.HIGHEST)
    row_part = jax.ops.segment_sum(to_rows, row_index, num_segments=panel_rows.shape[0])
    col_part = jax.ops.segment_sum(to_cols, col_index, num_segments=panel_cols.shape[0])
    return (row_part, col_part)


def fold_terms(row_part, col_part):
    return lax.psum_scatter(row_part, "col", scatter_dimension=0, tiled=True) + lax.psum_scatter(
        col_part, "row", scatter_dimension=0, tiled=True
    )


def total(field):
    return jnp.sum(field, axis=(0, 2))


def global_sum(partial_sum):
    return lax.psum(partial_sum, ("row", "col"))


def shards(block_values, block_index, block_count, strength, raw_scores):
    values = block_values[0, 0]
    row_index = block_index[0, 0, 0]
    col_index = block_index[0, 0, 1]
    live_mask = (jnp.arange(values.shape[0], dtype=jnp.int32) < block_count[0, 0]).astype(
        jnp.float32
    )
    masked = values * live_mask[:, None, None]
    segment = raw_scores.shape[0]
    block_size = raw_scores.shape[2]
    rows_here = lax.axis_size("col") * segment
    cols_here = lax.axis_size("row") * segment
    ones_rows = jnp.ones((rows_here, 1, block_size), jnp.float32)
    ones_cols = jnp.ones((cols_here, 1, block_size), jnp.float32)
    degree_rows, degree_cols = local_terms(masked, row_index, col_index, ones_rows, ones_cols)
    degree = fold_terms(degree_rows, degree_cols)
    gains = strength[None, :, None]
    smoothed = jnp.zeros_like(raw_scores)
    residual = raw_scores
    direction = raw_scores
    norm_now = global_sum(total(residual * residual))
    for iteration in range(ITERS):
        panel_rows = lax.all_gather(direction, "col", axis=0, tiled=True)
        panel_cols = lax.all_gather(direction, "row", axis=0, tiled=True)
        row_part, col_part = local_terms(masked, row_index, col_index, panel_rows, panel_cols)
        product = fold_terms(row_part, col_part)
        image = direction + gains * (degree * direction - product)
        step_size = norm_now / global_sum(total(direction * image))
        smoothed = smoothed + step_size[None, :, None] * direction
        residual = residual - step_size[None, :, None] * image
        norm_next = global_sum(total(residual * residual))
        direction = residual + (norm_next / norm_now)[None, :, None] * direction
        norm_now = norm_next
    return (smoothed, residual)


def solution(mesh):
    placed = (
        P("row", "col", None, None, None),
        P("row", "col", None, None),
        P("row", "col"),
        P(),
        P(("row", "col"), None, None),
    )
    return jax.shard_map(
        shards,
        mesh=mesh,
        in_specs=placed,
        out_specs=(P(("row", "col"), None, None), P(("row", "col"), None, None)),
        check_vma=False,
    )
```

profile of v0, /device:TPU:1, one launch (start us, length us, event | category | flops | bytes accessed | tf_op | source)
XLA Modules:
  0.0 916.9 jit_solution(5695150841030016190)
XLA Ops:
  7.2 0.8 compare_and_fusion
  8.0 0.8 slice_bitcast_fusion
  9.4 23.0 %all_gather.19 = f32[32,32,128]{2,1,0:T(8,128)S(1)} all-gather(f32[2,32,128]{2,1,0:T(8,128)} %param.13), channel_id=1, replica_groups=mesh['row'=16,'col'=16] {'col'}, dimensions={0}, use_global_device_ids=true | all-gather | bytes 557056 | tf_op jit(solution)/shard_map/all_gather | solution.py:55
  32.4 0.6 gather_fusion.3
  33.0 5.0 fusion.4
  38.1 4.9 scatter_fusion.1
  43.0 0.8 copy-done.3
  43.8 0.0 reduce-scatter.9.cloned.1.call-start
  43.9 19.6 %all_gather.18 = f32[32,32,128]{2,1,0:T(8,128)S(1)} all-gather(f32[2,32,128]{2,1,0:T(8,128)S(1)} %copy-done.7), channel_id=1, replica_groups=mesh['row'=16,'col'=16] {'row'}, dimensions={0}, use_global_device_ids=true | all-gather | bytes 557056 | tf_op jit(solution)/shard_map/all_gather | solution.py:56
  63.4 1.4 gather_fusion.2
  64.9 6.2 fusion.5
  71.1 4.7 scatter_fusion
  75.8 0.8 copy-done.4
  76.7 0.0 reduce-scatter.15.cloned.1.call-start
  76.7 0.6 gather_fusion
  77.3 0.6 gather_fusion.1
  77.9 0.6 dynamic-slice
  78.5 0.6 dynamic-slice.2
  80.4 0.1 bitcast_select_fusion
  80.5 4.3 fusion.7
  84.7 0.9 scatter_custom_fusion
  85.7 2.3 fusion.6
  88.0 0.7 scatter_custom_fusion.1
  88.7 58.4 %all-reduce.1 = f32[32,1,128]{2,0,1:T(8,128)S(1)} all-reduce(f32[32,1,128]{2,0,1:T(8,128)S(1)} %bitcast.49), channel_id=3, replica_groups=mesh['row'=16,'col'=16] {'row'}, use_global_device_ids=true, to_apply=%region_5.7.clone | all-reduce | flops 4096 | bytes 32768
  147.1 61.3 %all-reduce = f32[32,1,128]{2,0,1:T(8,128)S(1)} all-reduce(f32[32,1,128]{2,0,1:T(8,128)S(1)} %bitcast.48), channel_id=2, replica_groups=mesh['row'=16,'col'=16] {'col'}, use_global_device_ids=true, to_apply=%region_3.5.clone | all-reduce | flops 4096 | bytes 32768
  208.5 1.0 multiply_reduce_fusion.4
  209.5 74.0 %all-reduce.2 = (f32[32]{0:T(128)S(1)}, f32[32]{0:T(128)S(1)}) all-reduce(f32[32]{0:T(128)S(1)} %get-tuple-element.5, f32[32]{0:T(128)S(1)} %get-tuple-element.4), channel_id=1, replica_groups=mesh['row'=16,'col'=16] {'row','col'}, use_global_device_ids=true, to_apply=%region_1.2 | all-reduce | flops 64 | bytes 512 | tf_op jit(solution)/shard_map/psum | solution.py:30
  283.5 1.0 multiply_reduce_fusion.3
  284.5 74.5 %psum.44 = f32[32]{0:T(128)S(1)} all-reduce(f32[32]{0:T(128)S(1)} %get-tuple-element.10), channel_id=1, replica_groups=mesh['row'=16,'col'=16] {'row','col'}, use_global_device_ids=true, to_apply=%region_13.16 | all-reduce | flops 32 | bytes 256 | tf_op jit(solution)/shard_map/psum | solution.py:30
  358.9 0.1 multiply_add_fusion.4
  359.0 17.2 %all_gather.21 = f32[32,32,128]{2,1,0:T(8,128)S(1)} all-gather(f32[2,32,128]{2,1,0:T(8,128)S(1)} %multiply_add_fusion.4), channel_id=1, replica_groups=mesh['row'=16,'col'=16] {'col'}, dimensions={0}, use_global_device_ids=true | all-gather | bytes 557056 | tf_op jit(solution)/shard_map/all_gather | solution.py:55
  376.2 1.4 gather_fusion.5
  377.7 4.3 fusion.2
  382.1 4.7 scatter_fusion.3
  386.8 0.8 copy-done.5
  387.6 0.0 reduce-scatter.13.cloned.1.call-start
  387.7 19.2 %all_gather.20 = f32[32,32,128]{2,1,0:T(8,128)S(1)} all-gather(f32[2,32,128]{2,1,0:T(8,128)S(1)} %multiply_add_fusion.4), channel_id=1, replica_groups=mesh['row'=16,'col'=16] {'row'}, dimensions={0}, use_global_device_ids=true | all-gather | bytes 557056 | tf_op jit(solution)/shard_map/all_gather | solution.py:56
  406.8 1.4 gather_fusion.4
  408.3 6.2 fusion.3
  414.5 4.7 scatter_fusion.2
  419.2 0.8 copy-done.6
  420.1 38.4 %reduce-scatter.15.cloned.1.call-done = f32[2,32,128]{2,1,0:T(8,128)} async-done(((f32[32,32,128]{2,1,0:T(8,128)}), f32[2,32,128]{2,1,0:T(8,128)}) %reduce-scatter.15.cloned.1.call-update) | async-done | bytes 32784 | tf_op jit(solution)/shard_map/reduce_scatter | solution.py:20
  458.5 57.2 %reduce-scatter.13.cloned.1.call-done = f32[2,32,128]{2,1,0:T(8,128)} async-done(((f32[32,32,128]{2,1,0:T(8,128)}), f32[2,32,128]{2,1,0:T(8,128)}) %reduce-scatter.13.cloned.1.call-update) | async-done | bytes 32784 | tf_op jit(solution)/shard_map/reduce_scatter | solution.py:20
  515.7 1.0 multiply_reduce_fusion.2
  516.7 79.6 %psum.45 = f32[32]{0:T(128)S(1)} all-reduce(f32[32]{0:T(128)S(1)} %multiply_reduce_fusion.2), channel_id=1, replica_groups=mesh['row'=16,'col'=16] {'row','col'}, use_global_device_ids=true, to_apply=%region_19.22 | all-reduce | flops 32 | bytes 256 | tf_op jit(solution)/shard_map/psum | solution.py:30
  596.2 1.0 multiply_reduce_fusion.1
  597.2 72.4 %psum.46 = f32[32]{0:T(128)S(1)} all-reduce(f32[32]{0:T(128)S(1)} %get-tuple-element.8), channel_id=1, replica_groups=mesh['row'=16,'col'=16] {'row','col'}, use_global_device_ids=true, to_apply=%region_21.24 | all-reduce | flops 32 | bytes 256 | tf_op jit(solution)/shard_map/psum | solution.py:30
  669.6 0.1 multiply_add_fusion.2
  669.6 18.1 %all_gather.23 = f32[32,32,128]{2,1,0:T(8,128)S(1)} all-gather(f32[2,32,128]{2,1,0:T(8,128)S(1)} %multiply_add_fusion.2), channel_id=1, replica_groups=mesh['row'=16,'col'=16] {'col'}, dimensions={0}, use_global_device_ids=true | all-gather | bytes 557056 | tf_op jit(solution)/shard_map/all_gather | solution.py:55
  687.7 1.4 gather_fusion.7
  689.2 4.3 fusion
  693.6 4.7 scatter_fusion.5
  698.3 0.8 copy-done.2
  699.1 19.2 %all_gather.22 = f32[32,32,128]{2,1,0:T(8,128)S(1)} all-gather(f32[2,32,128]{2,1,0:T(8,128)S(1)} %multiply_add_fusion.2), channel_id=1, replica_groups=mesh['row'=16,'col'=16] {'row'}, dimensions={0}, use_global_device_ids=true | all-gather | bytes 557056 | tf_op jit(solution)/shard_map/all_gather | solution.py:56
  718.4 1.4 gather_fusion.6
  719.8 5.3 fusion.1
  725.1 0.1 broadcast.50.clone.4
  725.2 2.7 scatter_fusion.4
  727.9 0.8 copy-done.1
  728.7 41.8 %reduce-scatter.19.cloned.1.call-done = f32[2,32,128]{2,1,0:T(8,128)} async-done(((f32[32,32,128]{2,1,0:T(8,128)}), f32[2,32,128]{2,1,0:T(8,128)}) %reduce-scatter.19.cloned.1.call-update) | async-done | bytes 32784 | tf_op jit(solution)/shard_map/reduce_scatter | solution.py:20
  770.5 57.3 %reduce-scatter.17.cloned.1.call-done = f32[2,32,128]{2,1,0:T(8,128)} async-done(((f32[32,32,128]{2,1,0:T(8,128)}), f32[2,32,128]{2,1,0:T(8,128)}) %reduce-scatter.17.cloned.1.call-update) | async-done | bytes 32784 | tf_op jit(solution)/shard_map/reduce_scatter | solution.py:20
  827.8 1.0 multiply_reduce_fusion
  828.8 79.8 %psum.47 = f32[32]{0:T(128)S(1)} all-reduce(f32[32]{0:T(128)S(1)} %multiply_reduce_fusion), channel_id=1, replica_groups=mesh['row'=16,'col'=16] {'row','col'}, use_global_device_ids=true, to_apply=%region_27.30 | all-reduce | flops 32 | bytes 256 | tf_op jit(solution)/shard_map/psum | solution.py:30
  908.5 1.5 multiply_subtract_fusion
  (42 shorter events, 0.6 us)
Async XLA Ops:
  7.2 201.3 %reduce-scatter.11.cloned.1.call-start = ((), (), s32[]{:S(2)}) async-start(), calls=%async_computation.7 | async-start | bytes 557056 | tf_op jit(solution)/shard_map/reduce_scatter | solution.py:20
  33.0 10.9 %copy-start.7 = (f32[2,32,128]{2,1,0:T(8,128)S(1)}, f32[2,32,128]{2,1,0:T(8,128)}, u32[]{:S(2)}) copy-start(f32[2,32,128]{2,1,0:T(8,128)} %param.13) | copy-start | bytes 98308
  38.0 26.9 %copy-start = (f32[1,1,40,128,128]{4,3,2,1,0:T(8,128)S(1)}, f32[1,1,40,128,128]{4,3,2,1,0:T(8,128)}, u32[]{:S(2)}) copy-start(f32[1,1,40,128,128]{4,3,2,1,0:T(8,128)} %param.9) | copy-start | bytes 7864324
  42.9 0.8 copy-start.3
  43.8 164.7 %reduce-scatter.9.cloned.1.call-start = ((), (), s32[]{:S(2)}) async-start(), calls=%async_computation.6 | async-start | bytes 557056 | tf_op jit(solution)/shard_map/reduce_scatter | solution.py:20
  71.1 6.8 copy-start.10
  71.1 7.4 copy-start.9
  75.8 0.8 copy-start.4
  76.7 381.8 %reduce-scatter.15.cloned.1.call-start = ((), (), s32[]{:S(2)}) async-start(), calls=%async_computation.9 | async-start | bytes 557056 | tf_op jit(solution)/shard_map/reduce_scatter | solution.py:20
  80.4 128.1 %copy-start.8 = (f32[32]{0:T(128)S(1)}, f32[32]{0:T(128)}, u32[]{:S(2)}) copy-start(f32[32]{0:T(128)} %param.12) | copy-start | bytes 388
  386.8 0.8 copy-start.5
  387.6 128.1 %reduce-scatter.13.cloned.1.call-start = ((), (), s32[]{:S(2)}) async-start(), calls=%async_computation.8 | async-start | bytes 557056 | tf_op jit(solution)/shard_map/reduce_scatter | solution.py:20
  419.2 0.8 copy-start.6
  420.0 350.5 %reduce-scatter.19.cloned.1.call-start = ((), (), s32[]{:S(2)}) async-start(), calls=%async_computation.11 | async-start | bytes 557056 | tf_op jit(solution)/shard_map/reduce_scatter | solution.py:20
  698.3 0.8 copy-start.2
  699.1 128.7 %reduce-scatter.17.cloned.1.call-start = ((), (), s32[]{:S(2)}) async-start(), calls=%async_computation.10 | async-start | bytes 557056 | tf_op jit(solution)/shard_map/reduce_scatter | solution.py:20
  727.9 0.8 copy-start.1
Sparse Core Ops, SparseCore 0:
  43.9 73.4 reduce-scatter.10
  120.0 55.2 reduce-scatter.8
  387.7 70.6 reduce-scatter.14
  461.0 54.6 reduce-scatter.12
  699.2 71.2 reduce-scatter.18
  773.0 54.7 reduce-scatter.16
where the time goes:
time: 918 us; the launch traced here: 917 us
  blocking collectives  616 us (67%)
  waiting for transfers between devices  195 us (21%)
  matrix products  37.9 us (4%)
  other arithmetic  35.4 us (4%)
  between operations  16.3 us (2%)
  local copies, waits for them, and re-layouts  15.9 us (2%)
    psum x5, blocking collectives, global_sum(): return lax.psum(partial_sum, ('row', 'col'))  380 us
    unnamed x2, blocking collectives  120 us
    reduce_scatter x3, waiting for transfers between devices, fold_terms(): lax.psum_scatter(row_part, 'col', scatter_dimension=0, tiled=True)  115 us
    reduce_scatter x3, waiting for transfers between devices, fold_terms(): lax.psum_scatter(col_part, 'row', scatter_dimension=0, tiled=True)  80.2 us
    all_gather x3, blocking collectives, shards(): panel_rows = lax.all_gather(direction, 'col', axis=0, tiled=True)  58.3 us
    all_gather x3, blocking collectives, shards(): panel_cols = lax.all_gather(direction, 'row', axis=0, tiled=True)  58 us
    dot_general x4, matrix products, local_terms(): jnp.einsum('crk,cik->cri', picked_cols, values, precision=lax.Precision.H...  22 us
  transfers between devices with their start and end apart: 6, of which 4 were waited for; matrix products, arithmetic and copies ran while one was open for 5% of the time, Pallas kernels for 0%

commit v1 on v0

--- a/solution.py
+++ b/solution.py
@@ -27,7 +27,7 @@
 
 
 def global_sum(partial_sum):
-    return lax.psum(partial_sum, ("row", "col"))
+    return lax.psum(lax.psum(partial_sum, "row"), "col")
 
 
 def shards(block_values, block_index, block_count, strength, raw_scores):

time: 918 us -> 848 us (0.924)
  blocking collectives: 616 us -> 545 us
    psum x5 -> x10, blocking collectives: 380 us -> 315 us  [global_sum(): return lax.psum(lax.psum(partial_sum, 'row'), 'col')]
where the time goes in v1:
time: 848 us; the launch traced here: 847 us
  blocking collectives  545 us (64%)
  waiting for transfers between devices  195 us (23%)
  matrix products  37.9 us (4%)
  other arithmetic  35.4 us (4%)
  between operations  16.3 us (2%)
  local copies, waits for them, and re-layouts  15.9 us (2%)
    psum x10, blocking collectives, global_sum(): return lax.psum(lax.psum(partial_sum, 'row'), 'col')  315 us
    unnamed x2, blocking collectives  120 us
    reduce_scatter x3, waiting for transfers between devices, fold_terms(): lax.psum_scatter(row_part, 'col', scatter_dimension=0, tiled=True)  115 us
    reduce_scatter x3, waiting for transfers between devices, fold_terms(): lax.psum_scatter(col_part, 'row', scatter_dimension=0, tiled=True)  80.7 us
    all_gather x3, blocking collectives, shards(): panel_rows = lax.all_gather(direction, 'col', axis=0, tiled=True)  55.6 us
    all_gather x3, blocking collectives, shards(): panel_cols = lax.all_gather(direction, 'row', axis=0, tiled=True)  54.7 us
    dot_general x4, matrix products, local_terms(): jnp.einsum('crk,cik->cri', picked_cols, values, precision=lax.Precision.H...  22 us
  transfers between devices with their start and end apart: 6, of which 4 were waited for; matrix products, arithmetic and copies ran while one was open for 5% of the time, Pallas kernels for 0%

profile of v1, /device:TPU:1, one launch (start us, length us, event | category | flops | bytes accessed | tf_op | source)
XLA Modules:
  0.0 846.6 jit_solution(8864290569577856963)
XLA Ops:
  7.2 0.8 compare_and_fusion
  8.0 0.8 slice_bitcast_fusion
  9.4 23.0 %all_gather.19 = f32[32,32,128]{2,1,0:T(8,128)S(1)} all-gather(f32[2,32,128]{2,1,0:T(8,128)} %param.13), channel_id=1, replica_groups=mesh['row'=16,'col'=16] {'col'}, dimensions={0}, use_global_device_ids=true | all-gather | bytes 557056 | tf_op jit(solution)/shard_map/all_gather | solution.py:55
  32.4 0.6 gather_fusion.3
  33.0 5.0 fusion.4
  38.1 4.9 scatter_fusion.1
  43.0 0.8 copy-done.3
  43.9 19.6 %all_gather.18 = f32[32,32,128]{2,1,0:T(8,128)S(1)} all-gather(f32[2,32,128]{2,1,0:T(8,128)S(1)} %copy-done.7), channel_id=1, replica_groups=mesh['row'=16,'col'=16] {'row'}, dimensions={0}, use_global_device_ids=true | all-gather | bytes 557056 | tf_op jit(solution)/shard_map/all_gather | solution.py:56
  63.4 1.4 gather_fusion.2
  64.9 6.2 fusion.5
  71.1 4.7 scatter_fusion
  75.8 0.8 copy-done.4
  76.7 0.6 gather_fusion
  77.3 0.6 gather_fusion.1
  77.9 0.6 dynamic-slice
  78.5 0.6 dynamic-slice.2
  80.4 0.1 bitcast_select_fusion
  80.5 4.3 fusion.7
  84.7 0.9 scatter_custom_fusion
  85.7 2.3 fusion.6
  88.0 0.7 scatter_custom_fusion.1
  88.7 58.4 %all-reduce.1 = f32[32,1,128]{2,0,1:T(8,128)S(1)} all-reduce(f32[32,1,128]{2,0,1:T(8,128)S(1)} %bitcast.49), channel_id=3, replica_groups=mesh['row'=16,'col'=16] {'row'}, use_global_device_ids=true, to_apply=%region_6.8.clone | all-reduce | flops 4096 | bytes 32768
  147.1 61.3 %all-reduce = f32[32,1,128]{2,0,1:T(8,128)S(1)} all-reduce(f32[32,1,128]{2,0,1:T(8,128)S(1)} %bitcast.48), channel_id=2, replica_groups=mesh['row'=16,'col'=16] {'col'}, use_global_device_ids=true, to_apply=%region_4.6.clone | all-reduce | flops 4096 | bytes 32768
  208.5 1.0 multiply_reduce_fusion.4
  209.5 28.5 %all-reduce.3 = (f32[32]{0:T(128)S(1)}, f32[32]{0:T(128)S(1)}) all-reduce(f32[32]{0:T(128)S(1)} %get-tuple-element.5, f32[32]{0:T(128)S(1)} %get-tuple-element.4), channel_id=1, replica_groups=mesh['row'=16,'col'=16] {'row'}, use_global_device_ids=true, to_apply=%region_1.2 | all-reduce | flops 64 | bytes 512 | tf_op jit(solution)/shard_map/psum | solution.py:30
  238.0 33.4 %all-reduce.2 = (f32[32]{0:T(128)S(1)}, f32[32]{0:T(128)S(1)}) all-reduce(f32[32]{0:T(128)S(1)} %get-tuple-element.8, f32[32]{0:T(128)S(1)} %get-tuple-element.9), channel_id=1, replica_groups=mesh['row'=16,'col'=16] {'col'}, use_global_device_ids=true, to_apply=%region_2.3 | all-reduce | flops 64 | bytes 512 | tf_op jit(solution)/shard_map/psum | solution.py:30
  271.4 1.0 multiply_reduce_fusion.3
  272.3 30.2 %psum.88 = f32[32]{0:T(128)S(1)} all-reduce(f32[32]{0:T(128)S(1)} %get-tuple-element.12), channel_id=1, replica_groups=mesh['row'=16,'col'=16] {'row'}, use_global_device_ids=true, to_apply=%region_15.18 | all-reduce | flops 32 | bytes 256 | tf_op jit(solution)/shard_map/psum | solution.py:30
  302.5 30.8 %psum.89 = f32[32]{0:T(128)S(1)} all-reduce(f32[32]{0:T(128)S(1)} %psum.88), channel_id=1, replica_groups=mesh['row'=16,'col'=16] {'col'}, use_global_device_ids=true, to_apply=%region_16.19 | all-reduce | flops 32 | bytes 256 | tf_op jit(solution)/shard_map/psum | solution.py:30
  333.3 0.1 multiply_add_fusion.4
  333.4 16.2 %all_gather.21 = f32[32,32,128]{2,1,0:T(8,128)S(1)} all-gather(f32[2,32,128]{2,1,0:T(8,128)S(1)} %multiply_add_fusion.4), channel_id=1, replica_groups=mesh['row'=16,'col'=16] {'col'}, dimensions={0}, use_global_device_ids=true | all-gather | bytes 557056 | tf_op jit(solution)/shard_map/all_gather | solution.py:55
  349.6 1.4 gather_fusion.5
  351.0 4.3 fusion.2
  355.4 4.7 scatter_fusion.3
  360.1 0.8 copy-done.5
  361.0 16.7 %all_gather.20 = f32[32,32,128]{2,1,0:T(8,128)S(1)} all-gather(f32[2,32,128]{2,1,0:T(8,128)S(1)} %multiply_add_fusion.4), channel_id=1, replica_groups=mesh['row'=16,'col'=16] {'row'}, dimensions={0}, use_global_device_ids=true | all-gather | bytes 557056 | tf_op jit(solution)/shard_map/all_gather | solution.py:56
  377.7 1.4 gather_fusion.4
  379.2 6.2 fusion.3
  385.4 4.7 scatter_fusion.2
  390.1 0.8 copy-done.6
  391.0 38.7 %reduce-scatter.15.cloned.1.call-done = f32[2,32,128]{2,1,0:T(8,128)} async-done(((f32[32,32,128]{2,1,0:T(8,128)}), f32[2,32,128]{2,1,0:T(8,128)}) %reduce-scatter.15.cloned.1.call-update) | async-done | bytes 32784 | tf_op jit(solution)/shard_map/reduce_scatter | solution.py:20
  429.7 57.2 %reduce-scatter.13.cloned.1.call-done = f32[2,32,128]{2,1,0:T(8,128)} async-done(((f32[32,32,128]{2,1,0:T(8,128)}), f32[2,32,128]{2,1,0:T(8,128)}) %reduce-scatter.13.cloned.1.call-update) | async-done | bytes 32784 | tf_op jit(solution)/shard_map/reduce_scatter | solution.py:20
  486.9 1.0 multiply_reduce_fusion.2
  487.9 33.2 %psum.90 = f32[32]{0:T(128)S(1)} all-reduce(f32[32]{0:T(128)S(1)} %multiply_reduce_fusion.2), channel_id=1, replica_groups=mesh['row'=16,'col'=16] {'row'}, use_global_device_ids=true, to_apply=%region_22.25 | all-reduce | flops 32 | bytes 256 | tf_op jit(solution)/shard_map/psum | solution.py:30
  521.1 33.5 %psum.91 = f32[32]{0:T(128)S(1)} all-reduce(f32[32]{0:T(128)S(1)} %psum.90), channel_id=1, replica_groups=mesh['row'=16,'col'=16] {'col'}, use_global_device_ids=true, to_apply=%region_23.26 | all-reduce | flops 32 | bytes 256 | tf_op jit(solution)/shard_map/psum | solution.py:30
  554.6 1.0 multiply_reduce_fusion.1
  555.6 28.5 %psum.92 = f32[32]{0:T(128)S(1)} all-reduce(f32[32]{0:T(128)S(1)} %get-tuple-element.10), channel_id=1, replica_groups=mesh['row'=16,'col'=16] {'row'}, use_global_device_ids=true, to_apply=%region_25.28 | all-reduce | flops 32 | bytes 256 | tf_op jit(solution)/shard_map/psum | solution.py:30
  584.1 30.5 %psum.93 = f32[32]{0:T(128)S(1)} all-reduce(f32[32]{0:T(128)S(1)} %psum.92), channel_id=1, replica_groups=mesh['row'=16,'col'=16] {'col'}, use_global_device_ids=true, to_apply=%region_26.29 | all-reduce | flops 32 | bytes 256 | tf_op jit(solution)/shard_map/psum | solution.py:30
  614.7 16.4 %all_gather.23 = f32[32,32,128]{2,1,0:T(8,128)S(1)} all-gather(f32[2,32,128]{2,1,0:T(8,128)S(1)} %multiply_add_fusion.2), channel_id=1, replica_groups=mesh['row'=16,'col'=16] {'col'}, dimensions={0}, use_global_device_ids=true | all-gather | bytes 557056 | tf_op jit(solution)/shard_map/all_gather | solution.py:55
  631.1 1.4 gather_fusion.7
  632.5 4.3 fusion
  636.9 4.7 scatter_fusion.5
  641.6 0.8 copy-done.2
  642.5 18.5 %all_gather.22 = f32[32,32,128]{2,1,0:T(8,128)S(1)} all-gather(f32[2,32,128]{2,1,0:T(8,128)S(1)} %multiply_add_fusion.2), channel_id=1, replica_groups=mesh['row'=16,'col'=16] {'row'}, dimensions={0}, use_global_device_ids=true | all-gather | bytes 557056 | tf_op jit(solution)/shard_map/all_gather | solution.py:56
  660.9 1.4 gather_fusion.6
  662.4 5.3 fusion.1
  667.8 2.7 scatter_fusion.4
  670.5 0.8 copy-done.1
  671.3 42.0 %reduce-scatter.19.cloned.1.call-done = f32[2,32,128]{2,1,0:T(8,128)} async-done(((f32[32,32,128]{2,1,0:T(8,128)}), f32[2,32,128]{2,1,0:T(8,128)}) %reduce-scatter.19.cloned.1.call-update) | async-done | bytes 32784 | tf_op jit(solution)/shard_map/reduce_scatter | solution.py:20
  713.3 57.3 %reduce-scatter.17.cloned.1.call-done = f32[2,32,128]{2,1,0:T(8,128)} async-done(((f32[32,32,128]{2,1,0:T(8,128)}), f32[2,32,128]{2,1,0:T(8,128)}) %reduce-scatter.17.cloned.1.call-update) | async-done | bytes 32784 | tf_op jit(solution)/shard_map/reduce_scatter | solution.py:20
  770.5 1.0 multiply_reduce_fusion
  771.5 33.2 %psum.94 = f32[32]{0:T(128)S(1)} all-reduce(f32[32]{0:T(128)S(1)} %multiply_reduce_fusion), channel_id=1, replica_groups=mesh['row'=16,'col'=16] {'row'}, use_global_device_ids=true, to_apply=%region_32.35 | all-reduce | flops 32 | bytes 256 | tf_op jit(solution)/shard_map/psum | solution.py:30
  804.7 33.5 %psum.95 = f32[32]{0:T(128)S(1)} all-reduce(f32[32]{0:T(128)S(1)} %psum.94), channel_id=1, replica_groups=mesh['row'=16,'col'=16] {'col'}, use_global_device_ids=true, to_apply=%region_33.36 | all-reduce | flops 32 | bytes 256 | tf_op jit(solution)/shard_map/psum | solution.py:30
  838.2 1.5 multiply_subtract_fusion
  (47 shorter events, 0.8 us)
Async XLA Ops:
  7.2 201.3 %reduce-scatter.11.cloned.1.call-start = ((), (), s32[]{:S(2)}) async-start(), calls=%async_computation.7 | async-start | bytes 557056 | tf_op jit(solution)/shard_map/reduce_scatter | solution.py:20
  33.0 10.9 %copy-start.7 = (f32[2,32,128]{2,1,0:T(8,128)S(1)}, f32[2,32,128]{2,1,0:T(8,128)}, u32[]{:S(2)}) copy-start(f32[2,32,128]{2,1,0:T(8,128)} %param.13) | copy-start | bytes 98308
  38.0 26.9 %copy-start = (f32[1,1,40,128,128]{4,3,2,1,0:T(8,128)S(1)}, f32[1,1,40,128,128]{4,3,2,1,0:T(8,128)}, u32[]{:S(2)}) copy-start(f32[1,1,40,128,128]{4,3,2,1,0:T(8,128)} %param.9) | copy-start | bytes 7864324
  42.9 0.8 copy-start.3
  43.8 164.7 %reduce-scatter.9.cloned.1.call-start = ((), (), s32[]{:S(2)}) async-start(), calls=%async_computation.6 | async-start | bytes 557056 | tf_op jit(solution)/shard_map/reduce_scatter | solution.py:20
  71.1 6.8 copy-start.10
  71.1 7.4 copy-start.9
  75.8 0.8 copy-start.4
  76.7 353.0 %reduce-scatter.15.cloned.1.call-start = ((), (), s32[]{:S(2)}) async-start(), calls=%async_computation.9 | async-start | bytes 557056 | tf_op jit(solution)/shard_map/reduce_scatter | solution.py:20
  80.4 128.1 %copy-start.8 = (f32[32]{0:T(128)S(1)}, f32[32]{0:T(128)}, u32[]{:S(2)}) copy-start(f32[32]{0:T(128)} %param.12) | copy-start | bytes 388
  360.1 0.8 copy-start.5
  361.0 125.9 %reduce-scatter.13.cloned.1.call-start = ((), (), s32[]{:S(2)}) async-start(), calls=%async_computation.8 | async-start | bytes 557056 | tf_op jit(solution)/shard_map/reduce_scatter | solution.py:20
  390.1 0.8 copy-start.6
  390.9 322.3 %reduce-scatter.19.cloned.1.call-start = ((), (), s32[]{:S(2)}) async-start(), calls=%async_computation.11 | async-start | bytes 557056 | tf_op jit(solution)/shard_map/reduce_scatter | solution.py:20
  641.6 0.8 copy-start.2
  642.4 128.1 %reduce-scatter.17.cloned.1.call-start = ((), (), s32[]{:S(2)}) async-start(), calls=%async_computation.10 | async-start | bytes 557056 | tf_op jit(solution)/shard_map/reduce_scatter | solution.py:20
  670.4 0.8 copy-start.1
Sparse Core Ops, SparseCore 0:
  43.9 73.4 reduce-scatter.10
  120.0 55.2 reduce-scatter.8
  361.1 68.5 reduce-scatter.14
  432.2 54.6 reduce-scatter.12
  642.6 70.6 reduce-scatter.18
  715.8 54.7 reduce-scatter.16
